TPU v7x, 256 devices: a whole 4x4x8 slice. The times are simulated.
256 devices in a mesh: dom: 64 (over z, y, core), chan: 4 (over x).
Axes of the slice: x: 4, y: 4, z: 8, core: 2. Of those that a mesh axis runs over, the one named last changes fastest.
Arguments:
- features: bfloat16 [256, 65536], P('chan', 'dom'), may hold values from -6 to 6
- cotangent: bfloat16 [256, 65536], P('chan', 'dom'), may hold values from -6 to 6
- weights: bfloat16 [9, 256, 256], P(None, 'chan'), may hold values from -0.375 to 0.375
- tile_values: float32 [4096, 128, 128], P('dom'), may hold values from -0.046875 to 0.046875
- tile_cols: int32 [64, 8, 8], P('dom'), may hold values from 0 to 11, as said below
- send_list: int32 [64, 4, 128], P('dom'), may hold values from 0 to 1023
Outputs:
- input_grad: float32 [256, 65536], P('chan', 'dom')
- weight_grad: float32 [9, 256, 256], P(None, None, 'chan')
Inputs may be any that keep to these rules, and one draw needn't show every extreme that they name: `tile_cols`: values below 8 are blocks of the partition's own nodes; 8 + s is the block received from neighbour slot s. Tile 0 of row block r has column block r.
All inputs are finite; a program needn't handle non-finite values.
Results may differ from a plain program's by a relative error of at most 0.0003.
Values may be sent and summed in bfloat16 or wider, within the bound.
A program may use at most 128 MiB of HBM per device.

v0:
```python
import jax
import jax.numpy as jnp
from jax import lax
from jax.sharding import PartitionSpec as P

NEIGHBOUR_SHIFTS = (1, -1, 2, -2)


def from_behind(block, axis, distance):
    devices = range(lax.axis_size(axis))
    route = [((i - distance) % len(devices), i) for i in devices]
    return lax.ppermute(block, axis, route)


def exchange_rows(outgoing):
    received = [
        from_behind(outgoing[:, slot_index], "dom", offset)
        for slot_index, offset in enumerate(NEIGHBOUR_SHIFTS)
    ]
    return received


def apply_operator(field_in, tile_values, tile_cols, send_list):
    channels, local_nodes = field_in.shape
    tile_size = tile_values.shape[-1]
    per_row = tile_cols.shape[-1]
    outgoing = jnp.take(field_in, send_list[0], axis=1)
    received = exchange_rows(outgoing)
    extended = jnp.concatenate([field_in] + received, axis=1)
    blocks = extended.reshape(channels, -1, tile_size)
    picked = jnp.take(blocks, tile_cols.reshape(-1), axis=1)
    product = jnp.einsum("ctj,tjk->ctk", picked, tile_values, precision=lax.Precision.HIGHEST)
    return (
        product.reshape(channels, -1, per_row, tile_size).sum(axis=2).reshape(channels, local_nodes)
    )


def local(features, cotangent, weights, tile_values, tile_cols, send_list):
    top_order = weights.shape[0] - 1
    local_nodes = features.shape[1]

    def operator_on(field_in):
        return apply_operator(field_in, tile_values, tile_cols, send_list)

    feat_all, cot_all = (
        lax.all_gather(features, "chan", axis=0, tiled=True),
        lax.all_gather(cotangent, "chan", axis=0, tiled=True),
    )
    feat_wide = feat_all.astype(jnp.float32)

    def mixed_term(order_index):
        return jnp.dot(weights[order_index], cot_all, preferred_element_type=jnp.float32)

    def grad_term(state):
        return lax.dot_general(
            feat_wide, state, (((1,), (1,)), ((), ())), precision=lax.Precision.HIGHEST
        )

    cheb_prev = cotangent.astype(jnp.float32)
    grad_terms = [grad_term(cheb_prev)]
    cheb_now = operator_on(cheb_prev)
    grad_terms.append(grad_term(cheb_now))
    for order_index in range(2, top_order + 1):
        cheb_prev, cheb_now = (cheb_now, 2.0 * operator_on(cheb_now) - cheb_prev)
        grad_terms.append(grad_term(cheb_now))
    current = mixed_term(top_order)
    clen_later = jnp.zeros_like(current)
    for order_index in range(top_order - 1, 0, -1):
        current, clen_later = (
            mixed_term(order_index) + 2.0 * operator_on(current) - clen_later,
            current,
        )
    input_grad = mixed_term(0) + operator_on(current) - clen_later
    local_grads = jnp.stack(grad_terms)
    summed = lax.psum(local_grads, "dom")
    nodes_all = lax.axis_size("dom") * local_nodes
    return (input_grad, summed * float(nodes_all) ** (-0.5))


def solution(mesh):
    placed = (
        P("chan", "dom"),
        P("chan", "dom"),
        P(None, "chan", None),
        P("dom", None, None),
        P("dom", None, None),
        P("dom", None, None),
    )
    return jax.shard_map(
        local,
        mesh=mesh,
        in_specs=placed,
        out_specs=(P("chan", "dom"), P(None, None, "chan")),
        check_vma=False,
    )
```

profile of v0, /device:TPU:2, one launch (start us, length us, event | category | flops | bytes accessed | tf_op | source)
XLA Modules:
  0.0 664.3 jit_solution(9862079954037837758)
XLA Ops:
  8.6 13.7 %all_gather.6 = bf16[256,1024]{1,0:T(8,128)(2,1)S(1)} all-gather(bf16[64,1024]{1,0:T(8,128)(2,1)} %param.11), channel_id=1, replica_groups=mesh['dom'=64,'chan'=4] {'chan'}, dimensions={0}, use_global_device_ids=true | all-gather | bytes 655360 | tf_op jit(solution)/shard_map/all_gather | solution.py:47
  26.1 5.1 collective-permute-start.1
  31.2 5.3 collective-permute-start.3
  38.1 12.8 %all_gather.7 = bf16[256,1024]{1,0:T(8,128)(2,1)S(1)} all-gather(bf16[64,1024]{1,0:T(8,128)(2,1)S(1)} %copy-done.13), channel_id=1, replica_groups=mesh['dom'=64,'chan'=4] {'chan'}, dimensions={0}, use_global_device_ids=true | all-gather | bytes 655360 | tf_op jit(solution)/shard_map/all_gather | solution.py:46
  57.3 7.7 %collective-permute-done.34 = f32[64,128]{0,1:T(8,128)S(1)} collective-permute-done((f32[64,128]{0,1:T(8,128)S(1)}, f32[64,128]{0,1:T(8,128)S(1)}, u32[]{:S(2)}, u32[]{:S(2)}) %collective-permute-start.34) | collective-permute-done | bytes 32800 | tf_op jit(solution)/shard_map/ppermute | solution.py:12
  70.4 6.4 bitcast_reduce_fusion.7
  88.4 6.7 %bitcast_reduce_fusion.15 = f32[64,8,128]{2,0,1:T(8,128)S(1)} fusion(f32[64,128,128]{2,1,0:T(8,128)} %param.13, f32[64,64,128]{2,1,0:T(8,128)} %gather_fusion.1, pred[64]{0:T(512)(128)(4,1)S(1)} %compare_and_fusion), kind=kOutput, calls=%fused_computation.47 | convolution fusion | flops 806289408 | bytes 6553664 | tf_op jit(solution)/shard_map/ctj,tjk->ctk/dot_general | solution.py:32
  97.6 5.1 collective-permute-start.5
  102.7 5.3 collective-permute-start.7
  110.1 5.5 collective-permute-start.37
  115.6 5.3 collective-permute-start.39
  123.1 6.7 %bitcast_reduce_fusion.14 = f32[64,8,128]{2,0,1:T(8,128)S(1)} fusion(f32[64,128,128]{2,1,0:T(8,128)} %param.13, f32[64,64,128]{2,1,0:T(8,128)} %gather_fusion.3, pred[64]{0:T(512)(128)(4,1)S(1)} %compare_and_fusion), kind=kOutput, calls=%fused_computation.46 | convolution fusion | flops 806289408 | bytes 6553664 | tf_op jit(solution)/shard_map/ctj,tjk->ctk/dot_general | solution.py:32
  132.8 5.1 collective-permute-start.9
  140.8 5.5 collective-permute-start.11
  152.7 6.7 %bitcast_reduce_fusion.6 = f32[64,8,128]{2,0,1:T(8,128)S(1)} fusion(f32[64,128,128]{2,1,0:T(8,128)} %param.13, f32[64,64,128]{2,1,0:T(8,128)} %gather_fusion.19, pred[64]{0:T(512)(128)(4,1)S(1)} %compare_and_fusion), kind=kOutput, calls=%fused_computation.38 | convolution fusion | flops 806289408 | bytes 6553664 | tf_op jit(solution)/shard_map/ctj,tjk->ctk/dot_general | solution.py:32
  167.0 5.1 collective-permute-start.41
  172.1 5.5 collective-permute-start.43
  179.7 6.7 %bitcast_reduce_fusion.13 = f32[64,8,128]{2,0,1:T(8,128)S(1)} fusion(f32[64,128,128]{2,1,0:T(8,128)} %param.13, f32[64,64,128]{2,1,0:T(8,128)} %gather_fusion.5, pred[64]{0:T(512)(128)(4,1)S(1)} %compare_and_fusion), kind=kOutput, calls=%fused_computation.45 | convolution fusion | flops 806289408 | bytes 6553664 | tf_op jit(solution)/shard_map/ctj,tjk->ctk/dot_general | solution.py:32
  190.1 5.1 collective-permute-start.13
  198.1 5.6 collective-permute-start.15
  210.0 6.7 %bitcast_reduce_fusion.5 = f32[64,8,128]{2,0,1:T(8,128)S(1)} fusion(f32[64,128,128]{2,1,0:T(8,128)} %param.13, f32[64,64,128]{2,1,0:T(8,128)} %gather_fusion.21, pred[64]{0:T(512)(128)(4,1)S(1)} %compare_and_fusion), kind=kOutput, calls=%fused_computation.37 | convolution fusion | flops 806289408 | bytes 6553664 | tf_op jit(solution)/shard_map/ctj,tjk->ctk/dot_general | solution.py:32
  222.8 5.1 collective-permute-start.45
  230.5 5.8 collective-permute-start.47
  242.1 6.7 %bitcast_reduce_fusion.12 = f32[64,8,128]{2,0,1:T(8,128)S(1)} fusion(f32[64,128,128]{2,1,0:T(8,128)} %param.13, f32[64,64,128]{2,1,0:T(8,128)} %gather_fusion.7, pred[64]{0:T(512)(128)(4,1)S(1)} %compare_and_fusion), kind=kOutput, calls=%fused_computation.44 | convolution fusion | flops 806289408 | bytes 6553664 | tf_op jit(solution)/shard_map/ctj,tjk->ctk/dot_general | solution.py:32
  252.6 5.1 collective-permute-start.17
  259.7 5.5 collective-permute-start.19
  270.7 6.7 %bitcast_reduce_fusion.4 = f32[64,8,128]{2,0,1:T(8,128)S(1)} fusion(f32[64,128,128]{2,1,0:T(8,128)} %param.13, f32[64,64,128]{2,1,0:T(8,128)} %gather_fusion.23, pred[64]{0:T(512)(128)(4,1)S(1)} %compare_and_fusion), kind=kOutput, calls=%fused_computation.36 | convolution fusion | flops 806289408 | bytes 6553664 | tf_op jit(solution)/shard_map/ctj,tjk->ctk/dot_general | solution.py:32
  281.7 5.1 collective-permute-start.49
  288.3 5.5 collective-permute-start.51
  297.4 6.7 %bitcast_reduce_fusion.11 = f32[64,8,128]{2,0,1:T(8,128)S(1)} fusion(f32[64,128,128]{2,1,0:T(8,128)} %param.13, f32[64,64,128]{2,1,0:T(8,128)} %gather_fusion.9, pred[64]{0:T(512)(128)(4,1)S(1)} %compare_and_fusion), kind=kOutput, calls=%fused_computation.43 | convolution fusion | flops 806289408 | bytes 6553664 | tf_op jit(solution)/shard_map/ctj,tjk->ctk/dot_general | solution.py:32
  314.4 5.6 collective-permute-start.23
  325.5 6.7 %bitcast_reduce_fusion.3 = f32[64,8,128]{2,0,1:T(8,128)S(1)} fusion(f32[64,128,128]{2,1,0:T(8,128)} %param.13, f32[64,64,128]{2,1,0:T(8,128)} %gather_fusion.25, pred[64]{0:T(512)(128)(4,1)S(1)} %compare_and_fusion), kind=kOutput, calls=%fused_computation.35 | convolution fusion | flops 806289408 | bytes 6553664 | tf_op jit(solution)/shard_map/ctj,tjk->ctk/dot_general | solution.py:32
  336.4 5.1 collective-permute-start.53
  341.6 5.8 collective-permute-start.55
  349.5 6.7 %bitcast_reduce_fusion.10 = f32[64,8,128]{2,0,1:T(8,128)S(1)} fusion(f32[64,128,128]{2,1,0:T(8,128)} %param.13, f32[64,64,128]{2,1,0:T(8,128)} %gather_fusion.11, pred[64]{0:T(512)(128)(4,1)S(1)} %compare_and_fusion), kind=kOutput, calls=%fused_computation.42 | convolution fusion | flops 806289408 | bytes 6553664 | tf_op jit(solution)/shard_map/ctj,tjk->ctk/dot_general | solution.py:32
  359.9 5.1 collective-permute-start.25
  367.1 5.5 collective-permute-start.27
  378.1 6.7 %bitcast_reduce_fusion.2 = f32[64,8,128]{2,0,1:T(8,128)S(1)} fusion(f32[64,128,128]{2,1,0:T(8,128)} %param.13, f32[64,64,128]{2,1,0:T(8,128)} %gather_fusion.27, pred[64]{0:T(512)(128)(4,1)S(1)} %compare_and_fusion), kind=kOutput, calls=%fused_computation.34 | convolution fusion | flops 806289408 | bytes 6553664 | tf_op jit(solution)/shard_map/ctj,tjk->ctk/dot_general | solution.py:32
  389.0 5.1 collective-permute-start.57
  395.6 5.5 collective-permute-start.59
  404.7 6.7 %bitcast_reduce_fusion.9 = f32[64,8,128]{2,0,1:T(8,128)S(1)} fusion(f32[64,128,128]{2,1,0:T(8,128)} %param.13, f32[64,64,128]{2,1,0:T(8,128)} %gather_fusion.13, pred[64]{0:T(512)(128)(4,1)S(1)} %compare_and_fusion), kind=kOutput, calls=%fused_computation.41 | convolution fusion | flops 806289408 | bytes 6553664 | tf_op jit(solution)/shard_map/ctj,tjk->ctk/dot_general | solution.py:32
  415.2 5.1 collective-permute-start.29
  422.4 5.6 collective-permute-start.31
  433.5 6.7 %bitcast_reduce_fusion.1 = f32[64,8,128]{2,0,1:T(8,128)S(1)} fusion(f32[64,128,128]{2,1,0:T(8,128)} %param.13, f32[64,64,128]{2,1,0:T(8,128)} %gather_fusion.29, pred[64]{0:T(512)(128)(4,1)S(1)} %compare_and_fusion), kind=kOutput, calls=%fused_computation.33 | convolution fusion | flops 806289408 | bytes 6553664 | tf_op jit(solution)/shard_map/ctj,tjk->ctk/dot_general | solution.py:32
  450.4 5.6 collective-permute-start.63
  465.5 6.7 %bitcast_reduce_fusion = f32[64,8,128]{2,0,1:T(8,128)S(1)} fusion(f32[64,128,128]{2,1,0:T(8,128)} %param.13, f32[64,64,128]{2,1,0:T(8,128)} %gather_fusion.31, pred[64]{0:T(512)(128)(4,1)S(1)} %compare_and_fusion), kind=kOutput, calls=%fused_computation.32 | convolution fusion | flops 806289408 | bytes 6553664 | tf_op jit(solution)/shard_map/ctj,tjk->ctk/dot_general | solution.py:32
  473.8 6.7 %bitcast_reduce_fusion.8 = f32[64,8,128]{2,0,1:T(8,128)S(1)} fusion(f32[64,128,128]{2,1,0:T(8,128)} %param.13, f32[64,64,128]{2,1,0:T(8,128)} %gather_fusion.15, pred[64]{0:T(512)(128)(4,1)S(1)} %compare_and_fusion), kind=kOutput, calls=%fused_computation.40 | convolution fusion | flops 806289408 | bytes 6553664 | tf_op jit(solution)/shard_map/ctj,tjk->ctk/dot_general | solution.py:32
  482.2 172.9 %all-reduce.2.cloned.1.call-done = f32[9,256,64]{1,2,0:T(8,128)} async-done(((f32[9,256,64]{1,2,0:T(8,128)}), f32[9,256,64]{1,2,0:T(8,128)}) %all-reduce.2.cloned.1.call-update) | async-done | bytes 589840 | tf_op jit(solution)/shard_map/psum | solution.py:75
  (344 shorter events, 185.5 us)
Async XLA Ops:
  7.2 647.9 %all-reduce.2.cloned.1.call-start = ((), (), s32[]{:S(2)}) async-start(), calls=%async_computation | async-start | bytes 1179648 | tf_op jit(solution)/shard_map/psum | solution.py:75
  26.1 52.7 %collective-permute-start = (f32[64,128]{1,0:T(8,128)}, f32[64,128]{1,0:T(8,128)}, u32[]{:S(2)}, u32[]{:S(2)}) collective-permute-start(f32[64,128]{1,0:T(8,128)} %get-tuple-element.67), channel_id=1, source_target_pairs={{252,0},{0,4},{4,8},{8,12},{12,16},{16,20},{20,24},{24,28},{28,32}... | collective-permute-start | bytes 98312 | tf_op jit(solution)/shard_map/ppermute | solution.py:12
  26.1 54.0 %collective-permute-start.1 = (f32[64,128]{1,0:T(8,128)}, f32[64,128]{1,0:T(8,128)}, u32[]{:S(2)}, u32[]{:S(2)}) collective-permute-start(f32[64,128]{1,0:T(8,128)} %get-tuple-element.66), channel_id=1, source_target_pairs={{4,0},{8,4},{12,8},{16,12},{20,16},{24,20},{28,24},{32,28},{36,32}... | collective-permute-start | bytes 98312 | tf_op jit(solution)/shard_map/ppermute | solution.py:12
  31.2 50.4 %collective-permute-start.2 = (f32[64,128]{1,0:T(8,128)}, f32[64,128]{1,0:T(8,128)}, u32[]{:S(2)}, u32[]{:S(2)}) collective-permute-start(f32[64,128]{1,0:T(8,128)} %get-tuple-element.65), channel_id=1, source_target_pairs={{248,0},{252,4},{0,8},{4,12},{8,16},{12,20},{16,24},{20,28},{24,32... | collective-permute-start | bytes 98312 | tf_op jit(solution)/shard_map/ppermute | solution.py:12
  31.2 52.8 %collective-permute-start.3 = (f32[64,128]{1,0:T(8,128)}, f32[64,128]{1,0:T(8,128)}, u32[]{:S(2)}, u32[]{:S(2)}) collective-permute-start(f32[64,128]{1,0:T(8,128)} %get-tuple-element.64), channel_id=1, source_target_pairs={{8,0},{12,4},{16,8},{20,12},{24,16},{28,20},{32,24},{36,28},{40,32... | collective-permute-start | bytes 98312 | tf_op jit(solution)/shard_map/ppermute | solution.py:12
  110.1 29.3 %collective-permute-start.37 = (f32[64,128]{0,1:T(8,128)}, f32[64,128]{0,1:T(8,128)}, u32[]{:S(2)}, u32[]{:S(2)}) collective-permute-start(f32[64,128]{0,1:T(8,128)} %get-tuple-element.30), channel_id=1, source_target_pairs={{4,0},{8,4},{12,8},{16,12},{20,16},{24,20},{28,24},{32,28},{36,32}... | collective-permute-start | bytes 98312 | tf_op jit(solution)/shard_map/ppermute | solution.py:12
  115.6 32.1 %collective-permute-start.39 = (f32[64,128]{0,1:T(8,128)}, f32[64,128]{0,1:T(8,128)}, u32[]{:S(2)}, u32[]{:S(2)}) collective-permute-start(f32[64,128]{0,1:T(8,128)} %get-tuple-element.28), channel_id=1, source_target_pairs={{8,0},{12,4},{16,8},{20,12},{24,16},{28,20},{32,24},{36,28},{40,32... | collective-permute-start | bytes 98312 | tf_op jit(solution)/shard_map/ppermute | solution.py:12
  132.8 34.2 %collective-permute-start.8 = (f32[64,128]{1,0:T(8,128)}, f32[64,128]{1,0:T(8,128)S(1)}, u32[]{:S(2)}, u32[]{:S(2)}) collective-permute-start(f32[64,128]{1,0:T(8,128)} %get-tuple-element.59), channel_id=1, source_target_pairs={{252,0},{0,4},{4,8},{8,12},{12,16},{16,20},{20,24},{24,28},{28,32}... | collective-permute-start | bytes 98312 | tf_op jit(solution)/shard_map/ppermute | solution.py:12
  132.8 39.2 %collective-permute-start.9 = (f32[64,128]{1,0:T(8,128)}, f32[64,128]{1,0:T(8,128)S(1)}, u32[]{:S(2)}, u32[]{:S(2)}) collective-permute-start(f32[64,128]{1,0:T(8,128)} %get-tuple-element.58), channel_id=1, source_target_pairs={{4,0},{8,4},{12,8},{16,12},{20,16},{24,20},{28,24},{32,28},{36,32}... | collective-permute-start | bytes 98312 | tf_op jit(solution)/shard_map/ppermute | solution.py:12
  139.3 32.7 %collective-permute-start.10 = (f32[64,128]{1,0:T(8,128)}, f32[64,128]{1,0:T(8,128)S(1)}, u32[]{:S(2)}, u32[]{:S(2)}) collective-permute-start(f32[64,128]{1,0:T(8,128)} %get-tuple-element.57), channel_id=1, source_target_pairs={{248,0},{252,4},{0,8},{4,12},{8,16},{12,20},{16,24},{20,28},{24,32... | collective-permute-start | bytes 98312 | tf_op jit(solution)/shard_map/ppermute | solution.py:12
  140.8 36.8 %collective-permute-start.11 = (f32[64,128]{1,0:T(8,128)}, f32[64,128]{1,0:T(8,128)S(1)}, u32[]{:S(2)}, u32[]{:S(2)}) collective-permute-start(f32[64,128]{1,0:T(8,128)} %get-tuple-element.56), channel_id=1, source_target_pairs={{8,0},{12,4},{16,8},{20,12},{24,16},{28,20},{32,24},{36,28},{40,32... | collective-permute-start | bytes 98312 | tf_op jit(solution)/shard_map/ppermute | solution.py:12
  167.0 29.6 %collective-permute-start.41 = (f32[64,128]{0,1:T(8,128)}, f32[64,128]{0,1:T(8,128)}, u32[]{:S(2)}, u32[]{:S(2)}) collective-permute-start(f32[64,128]{0,1:T(8,128)} %get-tuple-element.26), channel_id=1, source_target_pairs={{4,0},{8,4},{12,8},{16,12},{20,16},{24,20},{28,24},{32,28},{36,32}... | collective-permute-start | bytes 98312 | tf_op jit(solution)/shard_map/ppermute | solution.py:12
  172.1 26.0 %collective-permute-start.42 = (f32[64,128]{0,1:T(8,128)}, f32[64,128]{0,1:T(8,128)}, u32[]{:S(2)}, u32[]{:S(2)}) collective-permute-start(f32[64,128]{0,1:T(8,128)} %get-tuple-element.25), channel_id=1, source_target_pairs={{248,0},{252,4},{0,8},{4,12},{8,16},{12,20},{16,24},{20,28},{24,32... | collective-permute-start | bytes 98312 | tf_op jit(solution)/shard_map/ppermute | solution.py:12
  172.1 33.0 %collective-permute-start.43 = (f32[64,128]{0,1:T(8,128)}, f32[64,128]{0,1:T(8,128)}, u32[]{:S(2)}, u32[]{:S(2)}) collective-permute-start(f32[64,128]{0,1:T(8,128)} %get-tuple-element.24), channel_id=1, source_target_pairs={{8,0},{12,4},{16,8},{20,12},{24,16},{28,20},{32,24},{36,28},{40,32... | collective-permute-start | bytes 98312 | tf_op jit(solution)/shard_map/ppermute | solution.py:12
  190.1 32.7 %collective-permute-start.12 = (f32[64,128]{1,0:T(8,128)S(1)}, f32[64,128]{1,0:T(8,128)S(1)}, u32[]{:S(2)}, u32[]{:S(2)}) collective-permute-start(f32[64,128]{1,0:T(8,128)S(1)} %get-tuple-element.55), channel_id=1, source_target_pairs={{252,0},{0,4},{4,8},{8,12},{12,16},{16,20},{20,24},{24,28},{28,32}... | collective-permute-start | bytes 98312 | tf_op jit(solution)/shard_map/ppermute | solution.py:12
  190.1 38.4 %collective-permute-start.13 = (f32[64,128]{1,0:T(8,128)}, f32[64,128]{1,0:T(8,128)S(1)}, u32[]{:S(2)}, u32[]{:S(2)}) collective-permute-start(f32[64,128]{1,0:T(8,128)} %get-tuple-element.54), channel_id=1, source_target_pairs={{4,0},{8,4},{12,8},{16,12},{20,16},{24,20},{28,24},{32,28},{36,32}... | collective-permute-start | bytes 98312 | tf_op jit(solution)/shard_map/ppermute | solution.py:12
  196.6 33.9 %collective-permute-start.14 = (f32[64,128]{1,0:T(8,128)}, f32[64,128]{1,0:T(8,128)}, u32[]{:S(2)}, u32[]{:S(2)}) collective-permute-start(f32[64,128]{1,0:T(8,128)} %get-tuple-element.53), channel_id=1, source_target_pairs={{248,0},{252,4},{0,8},{4,12},{8,16},{12,20},{16,24},{20,28},{24,32... | collective-permute-start | bytes 98312 | tf_op jit(solution)/shard_map/ppermute | solution.py:12
  198.1 39.6 %collective-permute-start.15 = (f32[64,128]{1,0:T(8,128)}, f32[64,128]{1,0:T(8,128)}, u32[]{:S(2)}, u32[]{:S(2)}) collective-permute-start(f32[64,128]{1,0:T(8,128)} %get-tuple-element.52), channel_id=1, source_target_pairs={{8,0},{12,4},{16,8},{20,12},{24,16},{28,20},{32,24},{36,28},{40,32... | collective-permute-start | bytes 98312 | tf_op jit(solution)/shard_map/ppermute | solution.py:12
  222.8 29.7 %collective-permute-start.44 = (f32[64,128]{0,1:T(8,128)}, f32[64,128]{0,1:T(8,128)}, u32[]{:S(2)}, u32[]{:S(2)}) collective-permute-start(f32[64,128]{0,1:T(8,128)} %get-tuple-element.23), channel_id=1, source_target_pairs={{252,0},{0,4},{4,8},{8,12},{12,16},{16,20},{20,24},{24,28},{28,32}... | collective-permute-start | bytes 98312 | tf_op jit(solution)/shard_map/ppermute | solution.py:12
  222.8 36.3 %collective-permute-start.45 = (f32[64,128]{0,1:T(8,128)}, f32[64,128]{0,1:T(8,128)S(1)}, u32[]{:S(2)}, u32[]{:S(2)}) collective-permute-start(f32[64,128]{0,1:T(8,128)} %get-tuple-element.22), channel_id=1, source_target_pairs={{4,0},{8,4},{12,8},{16,12},{20,16},{24,20},{28,24},{32,28},{36,32}... | collective-permute-start | bytes 98312 | tf_op jit(solution)/shard_map/ppermute | solution.py:12
  229.1 30.6 %collective-permute-start.46 = (f32[64,128]{0,1:T(8,128)}, f32[64,128]{0,1:T(8,128)S(1)}, u32[]{:S(2)}, u32[]{:S(2)}) collective-permute-start(f32[64,128]{0,1:T(8,128)} %get-tuple-element.21), channel_id=1, source_target_pairs={{248,0},{252,4},{0,8},{4,12},{8,16},{12,20},{16,24},{20,28},{24,32... | collective-permute-start | bytes 98312 | tf_op jit(solution)/shard_map/ppermute | solution.py:12
  230.5 35.3 %collective-permute-start.47 = (f32[64,128]{0,1:T(8,128)}, f32[64,128]{0,1:T(8,128)}, u32[]{:S(2)}, u32[]{:S(2)}) collective-permute-start(f32[64,128]{0,1:T(8,128)} %get-tuple-element.20), channel_id=1, source_target_pairs={{8,0},{12,4},{16,8},{20,12},{24,16},{28,20},{32,24},{36,28},{40,32... | collective-permute-start | bytes 98312 | tf_op jit(solution)/shard_map/ppermute | solution.py:12
  252.6 29.1 %collective-permute-start.16 = (f32[64,128]{1,0:T(8,128)}, f32[64,128]{1,0:T(8,128)}, u32[]{:S(2)}, u32[]{:S(2)}) collective-permute-start(f32[64,128]{1,0:T(8,128)} %get-tuple-element.51), channel_id=1, source_target_pairs={{252,0},{0,4},{4,8},{8,12},{12,16},{16,20},{20,24},{24,28},{28,32}... | collective-permute-start | bytes 98312 | tf_op jit(solution)/shard_map/ppermute | solution.py:12
  252.6 34.9 %collective-permute-start.17 = (f32[64,128]{1,0:T(8,128)}, f32[64,128]{1,0:T(8,128)}, u32[]{:S(2)}, u32[]{:S(2)}) collective-permute-start(f32[64,128]{1,0:T(8,128)} %get-tuple-element.50), channel_id=1, source_target_pairs={{4,0},{8,4},{12,8},{16,12},{20,16},{24,20},{28,24},{32,28},{36,32}... | collective-permute-start | bytes 98312 | tf_op jit(solution)/shard_map/ppermute | solution.py:12
  259.1 29.2 %collective-permute-start.18 = (f32[64,128]{1,0:T(8,128)}, f32[64,128]{1,0:T(8,128)}, u32[]{:S(2)}, u32[]{:S(2)}) collective-permute-start(f32[64,128]{1,0:T(8,128)} %get-tuple-element.49), channel_id=1, source_target_pairs={{248,0},{252,4},{0,8},{4,12},{8,16},{12,20},{16,24},{20,28},{24,32... | collective-permute-start | bytes 98312 | tf_op jit(solution)/shard_map/ppermute | solution.py:12
  259.7 34.8 %collective-permute-start.19 = (f32[64,128]{1,0:T(8,128)}, f32[64,128]{1,0:T(8,128)}, u32[]{:S(2)}, u32[]{:S(2)}) collective-permute-start(f32[64,128]{1,0:T(8,128)} %get-tuple-element.48), channel_id=1, source_target_pairs={{8,0},{12,4},{16,8},{20,12},{24,16},{28,20},{32,24},{36,28},{40,32... | collective-permute-start | bytes 98312 | tf_op jit(solution)/shard_map/ppermute | solution.py:12
  281.7 25.6 %collective-permute-start.48 = (f32[64,128]{0,1:T(8,128)}, f32[64,128]{0,1:T(8,128)}, u32[]{:S(2)}, u32[]{:S(2)}) collective-permute-start(f32[64,128]{0,1:T(8,128)} %get-tuple-element.19), channel_id=1, source_target_pairs={{252,0},{0,4},{4,8},{8,12},{12,16},{16,20},{20,24},{24,28},{28,32}... | collective-permute-start | bytes 98312 | tf_op jit(solution)/shard_map/ppermute | solution.py:12
  281.7 32.1 %collective-permute-start.49 = (f32[64,128]{0,1:T(8,128)}, f32[64,128]{0,1:T(8,128)S(1)}, u32[]{:S(2)}, u32[]{:S(2)}) collective-permute-start(f32[64,128]{0,1:T(8,128)} %get-tuple-element.18), channel_id=1, source_target_pairs={{4,0},{8,4},{12,8},{16,12},{20,16},{24,20},{28,24},{32,28},{36,32}... | collective-permute-start | bytes 98312 | tf_op jit(solution)/shard_map/ppermute | solution.py:12
  287.5 26.9 %collective-permute-start.50 = (f32[64,128]{0,1:T(8,128)}, f32[64,128]{0,1:T(8,128)S(1)}, u32[]{:S(2)}, u32[]{:S(2)}) collective-permute-start(f32[64,128]{0,1:T(8,128)} %get-tuple-element.17), channel_id=1, source_target_pairs={{248,0},{252,4},{0,8},{4,12},{8,16},{12,20},{16,24},{20,28},{24,32... | collective-permute-start | bytes 98312 | tf_op jit(solution)/shard_map/ppermute | solution.py:12
  288.3 32.4 %collective-permute-start.51 = (f32[64,128]{0,1:T(8,128)}, f32[64,128]{0,1:T(8,128)}, u32[]{:S(2)}, u32[]{:S(2)}) collective-permute-start(f32[64,128]{0,1:T(8,128)} %get-tuple-element.16), channel_id=1, source_target_pairs={{8,0},{12,4},{16,8},{20,12},{24,16},{28,20},{32,24},{36,28},{40,32... | collective-permute-start | bytes 98312 | tf_op jit(solution)/shard_map/ppermute | solution.py:12
  307.2 29.2 %collective-permute-start.20 = (f32[64,128]{1,0:T(8,128)S(1)}, f32[64,128]{1,0:T(8,128)S(1)}, u32[]{:S(2)}, u32[]{:S(2)}) collective-permute-start(f32[64,128]{1,0:T(8,128)S(1)} %get-tuple-element.47), channel_id=1, source_target_pairs={{252,0},{0,4},{4,8},{8,12},{12,16},{16,20},{20,24},{24,28},{28,32}... | collective-permute-start | bytes 98312 | tf_op jit(solution)/shard_map/ppermute | solution.py:12
  307.3 34.2 %collective-permute-start.21 = (f32[64,128]{1,0:T(8,128)S(1)}, f32[64,128]{1,0:T(8,128)S(1)}, u32[]{:S(2)}, u32[]{:S(2)}) collective-permute-start(f32[64,128]{1,0:T(8,128)S(1)} %get-tuple-element.46), channel_id=1, source_target_pairs={{4,0},{8,4},{12,8},{16,12},{20,16},{24,20},{28,24},{32,28},{36,32}... | collective-permute-start | bytes 98312 | tf_op jit(solution)/shard_map/ppermute | solution.py:12
  313.8 27.8 %collective-permute-start.22 = (f32[64,128]{1,0:T(8,128)S(1)}, f32[64,128]{1,0:T(8,128)S(1)}, u32[]{:S(2)}, u32[]{:S(2)}) collective-permute-start(f32[64,128]{1,0:T(8,128)S(1)} %get-tuple-element.45), channel_id=1, source_target_pairs={{248,0},{252,4},{0,8},{4,12},{8,16},{12,20},{16,24},{20,28},{24,32... | collective-permute-start | bytes 98312 | tf_op jit(solution)/shard_map/ppermute | solution.py:12
  314.4 33.0 %collective-permute-start.23 = (f32[64,128]{1,0:T(8,128)S(1)}, f32[64,128]{1,0:T(8,128)S(1)}, u32[]{:S(2)}, u32[]{:S(2)}) collective-permute-start(f32[64,128]{1,0:T(8,128)S(1)} %get-tuple-element.44), channel_id=1, source_target_pairs={{8,0},{12,4},{16,8},{20,12},{24,16},{28,20},{32,24},{36,28},{40,32... | collective-permute-start | bytes 98312 | tf_op jit(solution)/shard_map/ppermute | solution.py:12
  336.4 30.0 %collective-permute-start.53 = (f32[64,128]{0,1:T(8,128)}, f32[64,128]{0,1:T(8,128)S(1)}, u32[]{:S(2)}, u32[]{:S(2)}) collective-permute-start(f32[64,128]{0,1:T(8,128)} %get-tuple-element.14), channel_id=1, source_target_pairs={{4,0},{8,4},{12,8},{16,12},{20,16},{24,20},{28,24},{32,28},{36,32}... | collective-permute-start | bytes 98312 | tf_op jit(solution)/shard_map/ppermute | solution.py:12
  341.6 31.6 %collective-permute-start.55 = (f32[64,128]{0,1:T(8,128)}, f32[64,128]{0,1:T(8,128)}, u32[]{:S(2)}, u32[]{:S(2)}) collective-permute-start(f32[64,128]{0,1:T(8,128)} %get-tuple-element.12), channel_id=1, source_target_pairs={{8,0},{12,4},{16,8},{20,12},{24,16},{28,20},{32,24},{36,28},{40,32... | collective-permute-start | bytes 98312 | tf_op jit(solution)/shard_map/ppermute | solution.py:12
  359.9 29.1 %collective-permute-start.24 = (f32[64,128]{1,0:T(8,128)}, f32[64,128]{1,0:T(8,128)}, u32[]{:S(2)}, u32[]{:S(2)}) collective-permute-start(f32[64,128]{1,0:T(8,128)} %get-tuple-element.43), channel_id=1, source_target_pairs={{252,0},{0,4},{4,8},{8,12},{12,16},{16,20},{20,24},{24,28},{28,32}... | collective-permute-start | bytes 98312 | tf_op jit(solution)/shard_map/ppermute | solution.py:12
  359.9 34.9 %collective-permute-start.25 = (f32[64,128]{1,0:T(8,128)}, f32[64,128]{1,0:T(8,128)}, u32[]{:S(2)}, u32[]{:S(2)}) collective-permute-start(f32[64,128]{1,0:T(8,128)} %get-tuple-element.42), channel_id=1, source_target_pairs={{4,0},{8,4},{12,8},{16,12},{20,16},{24,20},{28,24},{32,28},{36,32}... | collective-permute-start | bytes 98312 | tf_op jit(solution)/shard_map/ppermute | solution.py:12
  366.5 29.1 %collective-permute-start.26 = (f32[64,128]{1,0:T(8,128)}, f32[64,128]{1,0:T(8,128)}, u32[]{:S(2)}, u32[]{:S(2)}) collective-permute-start(f32[64,128]{1,0:T(8,128)} %get-tuple-element.41), channel_id=1, source_target_pairs={{248,0},{252,4},{0,8},{4,12},{8,16},{12,20},{16,24},{20,28},{24,32... | collective-permute-start | bytes 98312 | tf_op jit(solution)/shard_map/ppermute | solution.py:12
  367.1 34.8 %collective-permute-start.27 = (f32[64,128]{1,0:T(8,128)}, f32[64,128]{1,0:T(8,128)}, u32[]{:S(2)}, u32[]{:S(2)}) collective-permute-start(f32[64,128]{1,0:T(8,128)} %get-tuple-element.40), channel_id=1, source_target_pairs={{8,0},{12,4},{16,8},{20,12},{24,16},{28,20},{32,24},{36,28},{40,32... | collective-permute-start | bytes 98312 | tf_op jit(solution)/shard_map/ppermute | solution.py:12
  389.0 26.2 %collective-permute-start.56 = (f32[64,128]{0,1:T(8,128)}, f32[64,128]{0,1:T(8,128)}, u32[]{:S(2)}, u32[]{:S(2)}) collective-permute-start(f32[64,128]{0,1:T(8,128)} %get-tuple-element.11), channel_id=1, source_target_pairs={{252,0},{0,4},{4,8},{8,12},{12,16},{16,20},{20,24},{24,28},{28,32}... | collective-permute-start | bytes 98312 | tf_op jit(solution)/shard_map/ppermute | solution.py:12
  389.0 32.7 %collective-permute-start.57 = (f32[64,128]{0,1:T(8,128)}, f32[64,128]{0,1:T(8,128)S(1)}, u32[]{:S(2)}, u32[]{:S(2)}) collective-permute-start(f32[64,128]{0,1:T(8,128)} %get-tuple-element.10), channel_id=1, source_target_pairs={{4,0},{8,4},{12,8},{16,12},{20,16},{24,20},{28,24},{32,28},{36,32}... | collective-permute-start | bytes 98312 | tf_op jit(solution)/shard_map/ppermute | solution.py:12
  394.8 27.5 %collective-permute-start.58 = (f32[64,128]{0,1:T(8,128)}, f32[64,128]{0,1:T(8,128)S(1)}, u32[]{:S(2)}, u32[]{:S(2)}) collective-permute-start(f32[64,128]{0,1:T(8,128)} %get-tuple-element.9), channel_id=1, source_target_pairs={{248,0},{252,4},{0,8},{4,12},{8,16},{12,20},{16,24},{20,28},{24,32... | collective-permute-start | bytes 98312 | tf_op jit(solution)/shard_map/ppermute | solution.py:12
  395.6 33.0 %collective-permute-start.59 = (f32[64,128]{0,1:T(8,128)}, f32[64,128]{0,1:T(8,128)}, u32[]{:S(2)}, u32[]{:S(2)}) collective-permute-start(f32[64,128]{0,1:T(8,128)} %get-tuple-element.8), channel_id=1, source_target_pairs={{8,0},{12,4},{16,8},{20,12},{24,16},{28,20},{32,24},{36,28},{40,32... | collective-permute-start | bytes 98312 | tf_op jit(solution)/shard_map/ppermute | solution.py:12
  415.2 28.6 %collective-permute-start.28 = (f32[64,128]{1,0:T(8,128)}, f32[64,128]{1,0:T(8,128)}, u32[]{:S(2)}, u32[]{:S(2)}) collective-permute-start(f32[64,128]{1,0:T(8,128)} %get-tuple-element.39), channel_id=1, source_target_pairs={{252,0},{0,4},{4,8},{8,12},{12,16},{16,20},{20,24},{24,28},{28,32}... | collective-permute-start | bytes 98312 | tf_op jit(solution)/shard_map/ppermute | solution.py:12
  415.2 34.4 %collective-permute-start.29 = (f32[64,128]{1,0:T(8,128)}, f32[64,128]{1,0:T(8,128)}, u32[]{:S(2)}, u32[]{:S(2)}) collective-permute-start(f32[64,128]{1,0:T(8,128)} %get-tuple-element.38), channel_id=1, source_target_pairs={{4,0},{8,4},{12,8},{16,12},{20,16},{24,20},{28,24},{32,28},{36,32}... | collective-permute-start | bytes 98312 | tf_op jit(solution)/shard_map/ppermute | solution.py:12
  421.7 28.6 %collective-permute-start.30 = (f32[64,128]{1,0:T(8,128)}, f32[64,128]{1,0:T(8,128)}, u32[]{:S(2)}, u32[]{:S(2)}) collective-permute-start(f32[64,128]{1,0:T(8,128)} %get-tuple-element.37), channel_id=1, source_target_pairs={{248,0},{252,4},{0,8},{4,12},{8,16},{12,20},{16,24},{20,28},{24,32... | collective-permute-start | bytes 98312 | tf_op jit(solution)/shard_map/ppermute | solution.py:12
  422.4 34.4 %collective-permute-start.31 = (f32[64,128]{1,0:T(8,128)}, f32[64,128]{1,0:T(8,128)}, u32[]{:S(2)}, u32[]{:S(2)}) collective-permute-start(f32[64,128]{1,0:T(8,128)} %get-tuple-element.36), channel_id=1, source_target_pairs={{8,0},{12,4},{16,8},{20,12},{24,16},{28,20},{32,24},{36,28},{40,32... | collective-permute-start | bytes 98312 | tf_op jit(solution)/shard_map/ppermute | solution.py:12
  (33 other events, 418.3 us)
Sparse Core Ops, SparseCore 0:
  473.9 181.1 all-reduce.1
where the time goes:
time: 673 us; the launch traced here: 664 us
  waiting for transfers between devices  187 us (28%)
  starting transfers between devices  164 us (24%)
  matrix products  131 us (19%)
  local copies, waits for them, and re-layouts  127 us (19%)
  blocking collectives  26.5 us (4%)
  between operations  15.7 us (2%)
  other arithmetic  13 us (2%)
    psum x1, waiting for transfers between devices, local(): summed = lax.psum(local_grads, 'dom')  173 us
    ppermute x64, starting transfers between devices, from_behind(): return lax.ppermute(block, axis, route)  163 us
    dot_general x16, matrix products, apply_operator(): jnp.einsum('ctj,tjk->ctk', picked, tile_values, precision=lax.Precision.H...  107 us
    unnamed x82, local copies, waits for them, and re-layouts  37.6 us
    gather x16, local copies, waits for them, and re-layouts, apply_operator(): picked = jnp.take(blocks, tile_cols.reshape(-1), axis=1)  31.3 us
    gather x24, local copies, waits for them, and re-layouts, apply_operator(): outgoing = jnp.take(field_in, send_list[0], axis=1)  18 us
    concatenate x16, local copies, waits for them, and re-layouts, apply_operator(): extended = jnp.concatenate([field_in] + received, axis=1)  14.5 us
    ppermute x64, waiting for transfers between devices, from_behind(): return lax.ppermute(block, axis, route)  14 us
  transfers between devices with their start and end apart: 65, of which 4 were waited for; matrix products, arithmetic and copies ran while one was open for 36% of the time, Pallas kernels for 0%

commit v1 on v0

--- a/solution.py
+++ b/solution.py
@@ -1,9 +1,23 @@
+import functools
 import jax
 import jax.numpy as jnp
 from jax import lax
 from jax.sharding import PartitionSpec as P
 
 NEIGHBOUR_SHIFTS = (1, -1, 2, -2)
+
+
+def obtain_leaves_up(sheet, dim_at):
+    tall = jnp.concatenate(
+        lax.all_to_all(
+            jnp.stack(tuple((sheet for _ in range(lax.axis_size("chan"))))), "chan", 0, 0
+        ),
+        axis=dim_at,
+    )
+    return tall
+
+
+recast_matrix_in = functools.partial(obtain_leaves_up, dim_at=0)
 
 
 def from_behind(block, axis, distance):
@@ -44,7 +58,7 @@
 
     feat_all, cot_all = (
         lax.all_gather(features, "chan", axis=0, tiled=True),
-        lax.all_gather(cotangent, "chan", axis=0, tiled=True),
+        recast_matrix_in(cotangent),
     )
     feat_wide = feat_all.astype(jnp.float32)
 

time: 673 us -> 611 us (0.908)
  local copies, waits for them, and re-layouts: 127 us -> 74.4 us
  blocking collectives: 26.5 us -> 13.4 us
  starting transfers between devices: 164 us -> 176 us
    unnamed x82 -> x80, local copies, waits for them, and re-layouts: 37.6 us -> 9.93 us
    all_gather x1 -> x0, blocking collectives: 13.7 us -> none  [local(): lax.all_gather(cotangent, 'chan', axis=0, tiled=True)]
    concatenate x16, local copies, waits for them, and re-layouts: 14.5 us -> 1.94 us  [apply_operator(): extended = jnp.concatenate([field_in] + received, axis=1)]
    psum x1, waiting for transfers between devices: 173 us -> 163 us  [local(): summed = lax.psum(local_grads, 'dom')]
    ppermute x64, waiting for transfers between devices: 14 us -> 22.3 us  [from_behind(): return lax.ppermute(block, axis, route)]
    squeeze x16, local copies, waits for them, and re-layouts: 8.17 us -> 0.91 us  [exchange_rows(): outgoing[:, slot_index]]
  transfers between devices with their start and end apart: 65 -> 66, of which waited for: 4 -> 18; matrix products, arithmetic and copies ran while one was open for 36% -> 26% of each run, Pallas kernels for 0% -> 0%
where the time goes in v1:
time: 611 us; the launch traced here: 602 us
  waiting for transfers between devices  185 us (30%)
  starting transfers between devices  176 us (29%)
  matrix products  126 us (21%)
  local copies, waits for them, and re-layouts  74.4 us (12%)
  between operations  15.8 us (3%)
  blocking collectives  13.4 us (2%)
  other arithmetic  11.6 us (2%)
    ppermute x64, starting transfers between devices, from_behind(): return lax.ppermute(block, axis, route)  170 us
    psum x1, waiting for transfers between devices, local(): summed = lax.psum(local_grads, 'dom')  163 us
    dot_general x16, matrix products, apply_operator(): jnp.einsum('ctj,tjk->ctk', picked, tile_values, precision=lax.Precision.H...  104 us
    gather x16, local copies, waits for them, and re-layouts, apply_operator(): picked = jnp.take(blocks, tile_cols.reshape(-1), axis=1)  27.1 us
    ppermute x64, waiting for transfers between devices, from_behind(): return lax.ppermute(block, axis, route)  22.3 us
    gather x24, local copies, waits for them, and re-layouts, apply_operator(): outgoing = jnp.take(field_in, send_list[0], axis=1)  20.6 us
    all_gather x1, blocking collectives, local(): lax.all_gather(features, 'chan', axis=0, tiled=True)  13.4 us
  transfers between devices with their start and end apart: 66, of which 18 were waited for; matrix products, arithmetic and copies ran while one was open for 26% of the time, Pallas kernels for 0%

profile of v1, /device:TPU:2, one launch (start us, length us, event | category | flops | bytes accessed | tf_op | source)
XLA Modules:
  0.0 602.3 jit_solution(6355846648055474403)
XLA Ops:
  9.0 5.7 all-to-all-start
  18.6 6.4 %collective-permute-start.33 = (f32[64,128]{0,1:T(8,128)S(1)}, f32[64,128]{0,1:T(8,128)S(1)}, u32[]{:S(2)}, u32[]{:S(2)}) collective-permute-start(f32[64,128]{0,1:T(8,128)S(1)} %get-tuple-element.34), channel_id=1, source_target_pairs={{4,0},{8,4},{12,8},{16,12},{20,16},{24,20},{28,24},{32,28},{36,32}... | collective-permute-start | bytes 98312 | tf_op jit(solution)/shard_map/ppermute | solution.py:26
  25.0 5.3 collective-permute-start.35
  30.4 13.4 %all_gather.3 = bf16[256,1024]{1,0:T(8,128)(2,1)S(1)} all-gather(bf16[64,1024]{1,0:T(8,128)(2,1)S(1)} %copy-done.13), channel_id=1, replica_groups=mesh['dom'=64,'chan'=4] {'chan'}, dimensions={0}, use_global_device_ids=true | all-gather | bytes 655360 | tf_op jit(solution)/shard_map/all_gather | solution.py:60
  45.8 6.4 %bitcast_reduce_fusion.7 = f32[64,8,128]{2,0,1:T(8,128)} fusion(f32[64,128,128]{2,1,0:T(8,128)} %param.13, f32[64,64,128]{2,1,0:T(8,128)S(1)} %gather_fusion.17, pred[64]{0:T(512)(128)(4,1)S(1)} %compare_and_fusion), kind=kOutput, calls=%fused_computation.39 | convolution fusion | flops 806289408 | bytes 6553664 | tf_op jit(solution)/shard_map/ctj,tjk->ctk/dot_general | solution.py:46
  55.9 5.1 collective-permute-start.37
  61.1 5.5 collective-permute-start.39
  71.0 6.7 %bitcast_reduce_fusion.6 = f32[64,8,128]{2,0,1:T(8,128)S(1)} fusion(f32[64,128,128]{2,1,0:T(8,128)} %param.13, f32[64,64,128]{2,1,0:T(8,128)} %gather_fusion.19, pred[64]{0:T(512)(128)(4,1)S(1)} %compare_and_fusion), kind=kOutput, calls=%fused_computation.38 | convolution fusion | flops 806289408 | bytes 6553664 | tf_op jit(solution)/shard_map/ctj,tjk->ctk/dot_general | solution.py:46
  82.4 5.0 collective-permute-start.41
  87.5 5.5 collective-permute-start.43
  97.3 6.7 %bitcast_reduce_fusion.5 = f32[64,8,128]{2,0,1:T(8,128)S(1)} fusion(f32[64,128,128]{2,1,0:T(8,128)} %param.13, f32[64,64,128]{2,1,0:T(8,128)} %gather_fusion.21, pred[64]{0:T(512)(128)(4,1)S(1)} %compare_and_fusion), kind=kOutput, calls=%fused_computation.37 | convolution fusion | flops 806289408 | bytes 6553664 | tf_op jit(solution)/shard_map/ctj,tjk->ctk/dot_general | solution.py:46
  108.8 5.0 collective-permute-start.45
  113.8 5.6 collective-permute-start.47
  123.7 6.7 %bitcast_reduce_fusion.4 = f32[64,8,128]{2,0,1:T(8,128)S(1)} fusion(f32[64,128,128]{2,1,0:T(8,128)} %param.13, f32[64,64,128]{2,1,0:T(8,128)} %gather_fusion.23, pred[64]{0:T(512)(128)(4,1)S(1)} %compare_and_fusion), kind=kOutput, calls=%fused_computation.36 | convolution fusion | flops 806289408 | bytes 6553664 | tf_op jit(solution)/shard_map/ctj,tjk->ctk/dot_general | solution.py:46
  134.1 5.0 collective-permute-start.49
  139.1 5.8 collective-permute-start.51
  151.4 6.7 %bitcast_reduce_fusion.3 = f32[64,8,128]{2,0,1:T(8,128)S(1)} fusion(f32[64,128,128]{2,1,0:T(8,128)} %param.13, f32[64,64,128]{2,1,0:T(8,128)} %gather_fusion.25, pred[64]{0:T(512)(128)(4,1)S(1)} %compare_and_fusion), kind=kOutput, calls=%fused_computation.35 | convolution fusion | flops 806289408 | bytes 6553664 | tf_op jit(solution)/shard_map/ctj,tjk->ctk/dot_general | solution.py:46
  161.7 5.0 collective-permute-start.53
  166.8 5.5 collective-permute-start.55
  179.0 6.7 %bitcast_reduce_fusion.2 = f32[64,8,128]{2,0,1:T(8,128)S(1)} fusion(f32[64,128,128]{2,1,0:T(8,128)} %param.13, f32[64,64,128]{2,1,0:T(8,128)} %gather_fusion.27, pred[64]{0:T(512)(128)(4,1)S(1)} %compare_and_fusion), kind=kOutput, calls=%fused_computation.34 | convolution fusion | flops 806289408 | bytes 6553664 | tf_op jit(solution)/shard_map/ctj,tjk->ctk/dot_general | solution.py:46
  189.4 5.0 collective-permute-start.57
  194.4 5.5 collective-permute-start.59
  204.3 6.7 %bitcast_reduce_fusion.1 = f32[64,8,128]{2,0,1:T(8,128)S(1)} fusion(f32[64,128,128]{2,1,0:T(8,128)} %param.13, f32[64,64,128]{2,1,0:T(8,128)} %gather_fusion.29, pred[64]{0:T(512)(128)(4,1)S(1)} %compare_and_fusion), kind=kOutput, calls=%fused_computation.33 | convolution fusion | flops 806289408 | bytes 6553664 | tf_op jit(solution)/shard_map/ctj,tjk->ctk/dot_general | solution.py:46
  216.3 5.1 collective-permute-start.61
  221.3 5.3 collective-permute-start.63
  236.7 5.6 collective-permute-start.3
  246.0 6.7 %bitcast_reduce_fusion.15 = f32[64,8,128]{2,0,1:T(8,128)S(1)} fusion(f32[64,128,128]{2,1,0:T(8,128)} %param.13, f32[64,64,128]{2,1,0:T(8,128)} %gather_fusion.1, pred[64]{0:T(512)(128)(4,1)S(1)} %compare_and_fusion), kind=kOutput, calls=%fused_computation.47 | convolution fusion | flops 806289408 | bytes 6553664 | tf_op jit(solution)/shard_map/ctj,tjk->ctk/dot_general | solution.py:46
  255.8 5.0 collective-permute-start.5
  260.8 5.5 collective-permute-start.7
  270.1 6.7 %bitcast_reduce_fusion.14 = f32[64,8,128]{2,0,1:T(8,128)S(1)} fusion(f32[64,128,128]{2,1,0:T(8,128)} %param.13, f32[64,64,128]{2,1,0:T(8,128)} %gather_fusion.3, pred[64]{0:T(512)(128)(4,1)S(1)} %compare_and_fusion), kind=kOutput, calls=%fused_computation.46 | convolution fusion | flops 806289408 | bytes 6553664 | tf_op jit(solution)/shard_map/ctj,tjk->ctk/dot_general | solution.py:46
  289.0 5.5 collective-permute-start.11
  298.3 6.7 %bitcast_reduce_fusion.13 = f32[64,8,128]{2,0,1:T(8,128)S(1)} fusion(f32[64,128,128]{2,1,0:T(8,128)} %param.13, f32[64,64,128]{2,1,0:T(8,128)} %gather_fusion.5, pred[64]{0:T(512)(128)(4,1)S(1)} %compare_and_fusion), kind=kOutput, calls=%fused_computation.45 | convolution fusion | flops 806289408 | bytes 6553664 | tf_op jit(solution)/shard_map/ctj,tjk->ctk/dot_general | solution.py:46
  307.5 6.7 %bitcast_reduce_fusion = f32[64,8,128]{2,0,1:T(8,128)S(1)} fusion(f32[64,128,128]{2,1,0:T(8,128)} %param.13, f32[64,64,128]{2,1,0:T(8,128)} %gather_fusion.31, pred[64]{0:T(512)(128)(4,1)S(1)} %compare_and_fusion), kind=kOutput, calls=%fused_computation.32 | convolution fusion | flops 806289408 | bytes 6553664 | tf_op jit(solution)/shard_map/ctj,tjk->ctk/dot_general | solution.py:46
  314.2 5.1 collective-permute-start.13
  319.3 5.7 collective-permute-start.15
  328.7 6.7 %bitcast_reduce_fusion.12 = f32[64,8,128]{2,0,1:T(8,128)S(1)} fusion(f32[64,128,128]{2,1,0:T(8,128)} %param.13, f32[64,64,128]{2,1,0:T(8,128)} %gather_fusion.7, pred[64]{0:T(512)(128)(4,1)S(1)} %compare_and_fusion), kind=kOutput, calls=%fused_computation.44 | convolution fusion | flops 806289408 | bytes 6553664 | tf_op jit(solution)/shard_map/ctj,tjk->ctk/dot_general | solution.py:46
  338.8 5.1 collective-permute-start.17
  344.0 5.5 collective-permute-start.19
  355.5 6.7 %bitcast_reduce_fusion.11 = f32[64,8,128]{2,0,1:T(8,128)S(1)} fusion(f32[64,128,128]{2,1,0:T(8,128)} %param.13, f32[64,64,128]{2,1,0:T(8,128)} %gather_fusion.9, pred[64]{0:T(512)(128)(4,1)S(1)} %compare_and_fusion), kind=kOutput, calls=%fused_computation.43 | convolution fusion | flops 806289408 | bytes 6553664 | tf_op jit(solution)/shard_map/ctj,tjk->ctk/dot_general | solution.py:46
  367.8 5.1 collective-permute-start.21
  372.9 5.3 collective-permute-start.23
  380.9 5.7 bitcast_reduce_fusion.10
  390.4 5.3 collective-permute-start.25
  395.7 5.3 collective-permute-start.27
  403.7 5.7 bitcast_reduce_fusion.9
  411.9 162.8 %all-reduce.2.cloned.1.call-done = f32[9,256,64]{1,2,0:T(8,128)} async-done(((f32[9,256,64]{1,2,0:T(8,128)}), f32[9,256,64]{1,2,0:T(8,128)}) %all-reduce.2.cloned.1.call-update) | async-done | bytes 589840 | tf_op jit(solution)/shard_map/psum | solution.py:89
  579.9 5.3 collective-permute-start.31
  587.9 5.7 bitcast_reduce_fusion.8
  (344 shorter events, 145.3 us)
Async XLA Ops:
  9.0 217.8 %all-to-all-start = ((bf16[4,64,1024]{2,1,0:T(8,128)(2,1)}), bf16[4,64,1024]{2,1,0:T(8,128)(2,1)S(1)}, u32[]{:S(2)}, u32[]{:S(2)}) async-start(bf16[4,64,1024]{2,1,0:T(8,128)(2,1)} %stack.37), calls=%async_computation | async-start | bytes 1048576 | tf_op jit(solution)/shard_map/all_to_all | solution.py:12
  14.7 560.0 %all-reduce.2.cloned.1.call-start = ((), (), s32[]{:S(2)}) async-start(), calls=%async_computation.1 | async-start | bytes 1179648 | tf_op jit(solution)/shard_map/psum | solution.py:89
  18.5 26.3 %collective-permute-start.32 = (f32[64,128]{0,1:T(8,128)S(1)}, f32[64,128]{0,1:T(8,128)S(1)}, u32[]{:S(2)}, u32[]{:S(2)}) collective-permute-start(f32[64,128]{0,1:T(8,128)S(1)} %get-tuple-element.35), channel_id=1, source_target_pairs={{252,0},{0,4},{4,8},{8,12},{12,16},{16,20},{20,24},{24,28},{28,32}... | collective-permute-start | bytes 98312 | tf_op jit(solution)/shard_map/ppermute | solution.py:26
  18.6 26.2 %collective-permute-start.33 = (f32[64,128]{0,1:T(8,128)S(1)}, f32[64,128]{0,1:T(8,128)S(1)}, u32[]{:S(2)}, u32[]{:S(2)}) collective-permute-start(f32[64,128]{0,1:T(8,128)S(1)} %get-tuple-element.34), channel_id=1, source_target_pairs={{4,0},{8,4},{12,8},{16,12},{20,16},{24,20},{28,24},{32,28},{36,32}... | collective-permute-start | bytes 98312 | tf_op jit(solution)/shard_map/ppermute | solution.py:26
  25.0 19.8 %collective-permute-start.34 = (f32[64,128]{0,1:T(8,128)S(1)}, f32[64,128]{0,1:T(8,128)S(1)}, u32[]{:S(2)}, u32[]{:S(2)}) collective-permute-start(f32[64,128]{0,1:T(8,128)S(1)} %get-tuple-element.33), channel_id=1, source_target_pairs={{248,0},{252,4},{0,8},{4,12},{8,16},{12,20},{16,24},{20,28},{24,32... | collective-permute-start | bytes 98312 | tf_op jit(solution)/shard_map/ppermute | solution.py:26
  25.0 19.8 %collective-permute-start.35 = (f32[64,128]{0,1:T(8,128)S(1)}, f32[64,128]{0,1:T(8,128)S(1)}, u32[]{:S(2)}, u32[]{:S(2)}) collective-permute-start(f32[64,128]{0,1:T(8,128)S(1)} %get-tuple-element.32), channel_id=1, source_target_pairs={{8,0},{12,4},{16,8},{20,12},{24,16},{28,20},{32,24},{36,28},{40,32... | collective-permute-start | bytes 98312 | tf_op jit(solution)/shard_map/ppermute | solution.py:26
  55.8 10.8 %collective-permute-start.36 = (f32[64,128]{0,1:T(8,128)S(1)}, f32[64,128]{0,1:T(8,128)S(1)}, u32[]{:S(2)}, u32[]{:S(2)}) collective-permute-start(f32[64,128]{0,1:T(8,128)S(1)} %get-tuple-element.31), channel_id=1, source_target_pairs={{252,0},{0,4},{4,8},{8,12},{12,16},{16,20},{20,24},{24,28},{28,32}... | collective-permute-start | bytes 98312 | tf_op jit(solution)/shard_map/ppermute | solution.py:26
  55.9 10.6 %collective-permute-start.37 = (f32[64,128]{0,1:T(8,128)S(1)}, f32[64,128]{0,1:T(8,128)S(1)}, u32[]{:S(2)}, u32[]{:S(2)}) collective-permute-start(f32[64,128]{0,1:T(8,128)S(1)} %get-tuple-element.30), channel_id=1, source_target_pairs={{4,0},{8,4},{12,8},{16,12},{20,16},{24,20},{28,24},{32,28},{36,32}... | collective-permute-start | bytes 98312 | tf_op jit(solution)/shard_map/ppermute | solution.py:26
  61.1 7.6 %collective-permute-start.39 = (f32[64,128]{0,1:T(8,128)S(1)}, f32[64,128]{0,1:T(8,128)S(1)}, u32[]{:S(2)}, u32[]{:S(2)}) collective-permute-start(f32[64,128]{0,1:T(8,128)S(1)} %get-tuple-element.28), channel_id=1, source_target_pairs={{8,0},{12,4},{16,8},{20,12},{24,16},{28,20},{32,24},{36,28},{40,32... | collective-permute-start | bytes 98312 | tf_op jit(solution)/shard_map/ppermute | solution.py:26
  81.1 11.9 %collective-permute-start.40 = (f32[64,128]{0,1:T(8,128)S(1)}, f32[64,128]{0,1:T(8,128)S(1)}, u32[]{:S(2)}, u32[]{:S(2)}) collective-permute-start(f32[64,128]{0,1:T(8,128)S(1)} %get-tuple-element.27), channel_id=1, source_target_pairs={{252,0},{0,4},{4,8},{8,12},{12,16},{16,20},{20,24},{24,28},{28,32}... | collective-permute-start | bytes 98312 | tf_op jit(solution)/shard_map/ppermute | solution.py:26
  82.4 10.6 %collective-permute-start.41 = (f32[64,128]{0,1:T(8,128)S(1)}, f32[64,128]{0,1:T(8,128)S(1)}, u32[]{:S(2)}, u32[]{:S(2)}) collective-permute-start(f32[64,128]{0,1:T(8,128)S(1)} %get-tuple-element.26), channel_id=1, source_target_pairs={{4,0},{8,4},{12,8},{16,12},{20,16},{24,20},{28,24},{32,28},{36,32}... | collective-permute-start | bytes 98312 | tf_op jit(solution)/shard_map/ppermute | solution.py:26
  87.5 7.6 %collective-permute-start.43 = (f32[64,128]{0,1:T(8,128)S(1)}, f32[64,128]{0,1:T(8,128)S(1)}, u32[]{:S(2)}, u32[]{:S(2)}) collective-permute-start(f32[64,128]{0,1:T(8,128)S(1)} %get-tuple-element.24), channel_id=1, source_target_pairs={{8,0},{12,4},{16,8},{20,12},{24,16},{28,20},{32,24},{36,28},{40,32... | collective-permute-start | bytes 98312 | tf_op jit(solution)/shard_map/ppermute | solution.py:26
  107.5 11.9 %collective-permute-start.44 = (f32[64,128]{0,1:T(8,128)S(1)}, f32[64,128]{0,1:T(8,128)S(1)}, u32[]{:S(2)}, u32[]{:S(2)}) collective-permute-start(f32[64,128]{0,1:T(8,128)S(1)} %get-tuple-element.23), channel_id=1, source_target_pairs={{252,0},{0,4},{4,8},{8,12},{12,16},{16,20},{20,24},{24,28},{28,32}... | collective-permute-start | bytes 98312 | tf_op jit(solution)/shard_map/ppermute | solution.py:26
  108.8 10.6 %collective-permute-start.45 = (f32[64,128]{0,1:T(8,128)S(1)}, f32[64,128]{0,1:T(8,128)S(1)}, u32[]{:S(2)}, u32[]{:S(2)}) collective-permute-start(f32[64,128]{0,1:T(8,128)S(1)} %get-tuple-element.22), channel_id=1, source_target_pairs={{4,0},{8,4},{12,8},{16,12},{20,16},{24,20},{28,24},{32,28},{36,32}... | collective-permute-start | bytes 98312 | tf_op jit(solution)/shard_map/ppermute | solution.py:26
  113.8 7.6 %collective-permute-start.46 = (f32[64,128]{0,1:T(8,128)S(1)}, f32[64,128]{0,1:T(8,128)S(1)}, u32[]{:S(2)}, u32[]{:S(2)}) collective-permute-start(f32[64,128]{0,1:T(8,128)S(1)} %get-tuple-element.21), channel_id=1, source_target_pairs={{248,0},{252,4},{0,8},{4,12},{8,16},{12,20},{16,24},{20,28},{24,32... | collective-permute-start | bytes 98312 | tf_op jit(solution)/shard_map/ppermute | solution.py:26
  113.8 7.6 %collective-permute-start.47 = (f32[64,128]{0,1:T(8,128)S(1)}, f32[64,128]{0,1:T(8,128)S(1)}, u32[]{:S(2)}, u32[]{:S(2)}) collective-permute-start(f32[64,128]{0,1:T(8,128)S(1)} %get-tuple-element.20), channel_id=1, source_target_pairs={{8,0},{12,4},{16,8},{20,12},{24,16},{28,20},{32,24},{36,28},{40,32... | collective-permute-start | bytes 98312 | tf_op jit(solution)/shard_map/ppermute | solution.py:26
  132.7 12.2 %collective-permute-start.48 = (f32[64,128]{0,1:T(8,128)S(1)}, f32[64,128]{0,1:T(8,128)S(1)}, u32[]{:S(2)}, u32[]{:S(2)}) collective-permute-start(f32[64,128]{0,1:T(8,128)S(1)} %get-tuple-element.19), channel_id=1, source_target_pairs={{252,0},{0,4},{4,8},{8,12},{12,16},{16,20},{20,24},{24,28},{28,32}... | collective-permute-start | bytes 98312 | tf_op jit(solution)/shard_map/ppermute | solution.py:26
  134.1 11.5 %collective-permute-start.49 = (f32[64,128]{0,1:T(8,128)S(1)}, f32[64,128]{0,1:T(8,128)S(1)}, u32[]{:S(2)}, u32[]{:S(2)}) collective-permute-start(f32[64,128]{0,1:T(8,128)S(1)} %get-tuple-element.18), channel_id=1, source_target_pairs={{4,0},{8,4},{12,8},{16,12},{20,16},{24,20},{28,24},{32,28},{36,32}... | collective-permute-start | bytes 98312 | tf_op jit(solution)/shard_map/ppermute | solution.py:26
  139.1 7.6 %collective-permute-start.50 = (f32[64,128]{0,1:T(8,128)S(1)}, f32[64,128]{0,1:T(8,128)S(1)}, u32[]{:S(2)}, u32[]{:S(2)}) collective-permute-start(f32[64,128]{0,1:T(8,128)S(1)} %get-tuple-element.17), channel_id=1, source_target_pairs={{248,0},{252,4},{0,8},{4,12},{8,16},{12,20},{16,24},{20,28},{24,32... | collective-permute-start | bytes 98312 | tf_op jit(solution)/shard_map/ppermute | solution.py:26
  139.1 8.2 %collective-permute-start.51 = (f32[64,128]{0,1:T(8,128)S(1)}, f32[64,128]{0,1:T(8,128)S(1)}, u32[]{:S(2)}, u32[]{:S(2)}) collective-permute-start(f32[64,128]{0,1:T(8,128)S(1)} %get-tuple-element.16), channel_id=1, source_target_pairs={{8,0},{12,4},{16,8},{20,12},{24,16},{28,20},{32,24},{36,28},{40,32... | collective-permute-start | bytes 98312 | tf_op jit(solution)/shard_map/ppermute | solution.py:26
  160.4 11.9 %collective-permute-start.52 = (f32[64,128]{0,1:T(8,128)S(1)}, f32[64,128]{0,1:T(8,128)S(1)}, u32[]{:S(2)}, u32[]{:S(2)}) collective-permute-start(f32[64,128]{0,1:T(8,128)S(1)} %get-tuple-element.15), channel_id=1, source_target_pairs={{252,0},{0,4},{4,8},{8,12},{12,16},{16,20},{20,24},{24,28},{28,32}... | collective-permute-start | bytes 98312 | tf_op jit(solution)/shard_map/ppermute | solution.py:26
  161.7 11.2 %collective-permute-start.53 = (f32[64,128]{0,1:T(8,128)S(1)}, f32[64,128]{0,1:T(8,128)S(1)}, u32[]{:S(2)}, u32[]{:S(2)}) collective-permute-start(f32[64,128]{0,1:T(8,128)S(1)} %get-tuple-element.14), channel_id=1, source_target_pairs={{4,0},{8,4},{12,8},{16,12},{20,16},{24,20},{28,24},{32,28},{36,32}... | collective-permute-start | bytes 98312 | tf_op jit(solution)/shard_map/ppermute | solution.py:26
  166.8 7.6 %collective-permute-start.54 = (f32[64,128]{0,1:T(8,128)S(1)}, f32[64,128]{0,1:T(8,128)S(1)}, u32[]{:S(2)}, u32[]{:S(2)}) collective-permute-start(f32[64,128]{0,1:T(8,128)S(1)} %get-tuple-element.13), channel_id=1, source_target_pairs={{248,0},{252,4},{0,8},{4,12},{8,16},{12,20},{16,24},{20,28},{24,32... | collective-permute-start | bytes 98312 | tf_op jit(solution)/shard_map/ppermute | solution.py:26
  166.8 8.2 %collective-permute-start.55 = (f32[64,128]{0,1:T(8,128)S(1)}, f32[64,128]{0,1:T(8,128)S(1)}, u32[]{:S(2)}, u32[]{:S(2)}) collective-permute-start(f32[64,128]{0,1:T(8,128)S(1)} %get-tuple-element.12), channel_id=1, source_target_pairs={{8,0},{12,4},{16,8},{20,12},{24,16},{28,20},{32,24},{36,28},{40,32... | collective-permute-start | bytes 98312 | tf_op jit(solution)/shard_map/ppermute | solution.py:26
  188.1 11.9 %collective-permute-start.56 = (f32[64,128]{0,1:T(8,128)S(1)}, f32[64,128]{0,1:T(8,128)S(1)}, u32[]{:S(2)}, u32[]{:S(2)}) collective-permute-start(f32[64,128]{0,1:T(8,128)S(1)} %get-tuple-element.11), channel_id=1, source_target_pairs={{252,0},{0,4},{4,8},{8,12},{12,16},{16,20},{20,24},{24,28},{28,32}... | collective-permute-start | bytes 98312 | tf_op jit(solution)/shard_map/ppermute | solution.py:26
  189.4 10.6 %collective-permute-start.57 = (f32[64,128]{0,1:T(8,128)S(1)}, f32[64,128]{0,1:T(8,128)S(1)}, u32[]{:S(2)}, u32[]{:S(2)}) collective-permute-start(f32[64,128]{0,1:T(8,128)S(1)} %get-tuple-element.10), channel_id=1, source_target_pairs={{4,0},{8,4},{12,8},{16,12},{20,16},{24,20},{28,24},{32,28},{36,32}... | collective-permute-start | bytes 98312 | tf_op jit(solution)/shard_map/ppermute | solution.py:26
  194.4 7.6 %collective-permute-start.58 = (f32[64,128]{0,1:T(8,128)S(1)}, f32[64,128]{0,1:T(8,128)S(1)}, u32[]{:S(2)}, u32[]{:S(2)}) collective-permute-start(f32[64,128]{0,1:T(8,128)S(1)} %get-tuple-element.9), channel_id=1, source_target_pairs={{248,0},{252,4},{0,8},{4,12},{8,16},{12,20},{16,24},{20,28},{24,32... | collective-permute-start | bytes 98312 | tf_op jit(solution)/shard_map/ppermute | solution.py:26
  194.4 7.6 %collective-permute-start.59 = (f32[64,128]{0,1:T(8,128)S(1)}, f32[64,128]{0,1:T(8,128)S(1)}, u32[]{:S(2)}, u32[]{:S(2)}) collective-permute-start(f32[64,128]{0,1:T(8,128)S(1)} %get-tuple-element.8), channel_id=1, source_target_pairs={{8,0},{12,4},{16,8},{20,12},{24,16},{28,20},{32,24},{36,28},{40,32... | collective-permute-start | bytes 98312 | tf_op jit(solution)/shard_map/ppermute | solution.py:26
  215.1 11.6 %collective-permute-start.60 = (f32[64,128]{0,1:T(8,128)S(1)}, f32[64,128]{0,1:T(8,128)S(1)}, u32[]{:S(2)}, u32[]{:S(2)}) collective-permute-start(f32[64,128]{0,1:T(8,128)S(1)} %get-tuple-element.7), channel_id=1, source_target_pairs={{252,0},{0,4},{4,8},{8,12},{12,16},{16,20},{20,24},{24,28},{28,32}... | collective-permute-start | bytes 98312 | tf_op jit(solution)/shard_map/ppermute | solution.py:26
  216.3 13.8 %collective-permute-start.61 = (f32[64,128]{0,1:T(8,128)}, f32[64,128]{0,1:T(8,128)}, u32[]{:S(2)}, u32[]{:S(2)}) collective-permute-start(f32[64,128]{0,1:T(8,128)} %get-tuple-element.6), channel_id=1, source_target_pairs={{4,0},{8,4},{12,8},{16,12},{20,16},{24,20},{28,24},{32,28},{36,32}... | collective-permute-start | bytes 98312 | tf_op jit(solution)/shard_map/ppermute | solution.py:26
  221.3 33.8 %collective-permute-start.62 = (f32[64,128]{0,1:T(8,128)}, f32[64,128]{0,1:T(8,128)S(1)}, u32[]{:S(2)}, u32[]{:S(2)}) collective-permute-start(f32[64,128]{0,1:T(8,128)} %get-tuple-element.5), channel_id=1, source_target_pairs={{248,0},{252,4},{0,8},{4,12},{8,16},{12,20},{16,24},{20,28},{24,32... | collective-permute-start | bytes 98312 | tf_op jit(solution)/shard_map/ppermute | solution.py:26
  221.3 60.2 %collective-permute-start.63 = (f32[64,128]{0,1:T(8,128)}, f32[64,128]{0,1:T(8,128)S(1)}, u32[]{:S(2)}, u32[]{:S(2)}) collective-permute-start(f32[64,128]{0,1:T(8,128)} %get-tuple-element.4), channel_id=1, source_target_pairs={{8,0},{12,4},{16,8},{20,12},{24,16},{28,20},{32,24},{36,28},{40,32... | collective-permute-start | bytes 98312 | tf_op jit(solution)/shard_map/ppermute | solution.py:26
  231.5 10.8 %collective-permute-start.1 = (f32[64,128]{1,0:T(8,128)S(1)}, f32[64,128]{1,0:T(8,128)S(1)}, u32[]{:S(2)}, u32[]{:S(2)}) collective-permute-start(f32[64,128]{1,0:T(8,128)S(1)} %get-tuple-element.66), channel_id=1, source_target_pairs={{4,0},{8,4},{12,8},{16,12},{20,16},{24,20},{28,24},{32,28},{36,32}... | collective-permute-start | bytes 98312 | tf_op jit(solution)/shard_map/ppermute | solution.py:26
  255.1 11.3 %collective-permute-start.4 = (f32[64,128]{1,0:T(8,128)S(1)}, f32[64,128]{1,0:T(8,128)S(1)}, u32[]{:S(2)}, u32[]{:S(2)}) collective-permute-start(f32[64,128]{1,0:T(8,128)S(1)} %get-tuple-element.63), channel_id=1, source_target_pairs={{252,0},{0,4},{4,8},{8,12},{12,16},{16,20},{20,24},{24,28},{28,32}... | collective-permute-start | bytes 98312 | tf_op jit(solution)/shard_map/ppermute | solution.py:26
  255.8 10.6 %collective-permute-start.5 = (f32[64,128]{1,0:T(8,128)S(1)}, f32[64,128]{1,0:T(8,128)S(1)}, u32[]{:S(2)}, u32[]{:S(2)}) collective-permute-start(f32[64,128]{1,0:T(8,128)S(1)} %get-tuple-element.62), channel_id=1, source_target_pairs={{4,0},{8,4},{12,8},{16,12},{20,16},{24,20},{28,24},{32,28},{36,32}... | collective-permute-start | bytes 98312 | tf_op jit(solution)/shard_map/ppermute | solution.py:26
  281.5 13.0 %collective-permute-start.8 = (f32[64,128]{1,0:T(8,128)S(1)}, f32[64,128]{1,0:T(8,128)S(1)}, u32[]{:S(2)}, u32[]{:S(2)}) collective-permute-start(f32[64,128]{1,0:T(8,128)S(1)} %get-tuple-element.59), channel_id=1, source_target_pairs={{252,0},{0,4},{4,8},{8,12},{12,16},{16,20},{20,24},{24,28},{28,32}... | collective-permute-start | bytes 98312 | tf_op jit(solution)/shard_map/ppermute | solution.py:26
  283.9 10.6 %collective-permute-start.9 = (f32[64,128]{1,0:T(8,128)S(1)}, f32[64,128]{1,0:T(8,128)S(1)}, u32[]{:S(2)}, u32[]{:S(2)}) collective-permute-start(f32[64,128]{1,0:T(8,128)S(1)} %get-tuple-element.58), channel_id=1, source_target_pairs={{4,0},{8,4},{12,8},{16,12},{20,16},{24,20},{28,24},{32,28},{36,32}... | collective-permute-start | bytes 98312 | tf_op jit(solution)/shard_map/ppermute | solution.py:26
  307.4 17.6 %collective-permute-start.12 = (f32[64,128]{1,0:T(8,128)S(1)}, f32[64,128]{1,0:T(8,128)S(1)}, u32[]{:S(2)}, u32[]{:S(2)}) collective-permute-start(f32[64,128]{1,0:T(8,128)S(1)} %get-tuple-element.55), channel_id=1, source_target_pairs={{252,0},{0,4},{4,8},{8,12},{12,16},{16,20},{20,24},{24,28},{28,32}... | collective-permute-start | bytes 98312 | tf_op jit(solution)/shard_map/ppermute | solution.py:26
  314.2 10.9 %collective-permute-start.13 = (f32[64,128]{1,0:T(8,128)S(1)}, f32[64,128]{1,0:T(8,128)S(1)}, u32[]{:S(2)}, u32[]{:S(2)}) collective-permute-start(f32[64,128]{1,0:T(8,128)S(1)} %get-tuple-element.54), channel_id=1, source_target_pairs={{4,0},{8,4},{12,8},{16,12},{20,16},{24,20},{28,24},{32,28},{36,32}... | collective-permute-start | bytes 98312 | tf_op jit(solution)/shard_map/ppermute | solution.py:26
  338.5 11.0 %collective-permute-start.16 = (f32[64,128]{1,0:T(8,128)S(1)}, f32[64,128]{1,0:T(8,128)S(1)}, u32[]{:S(2)}, u32[]{:S(2)}) collective-permute-start(f32[64,128]{1,0:T(8,128)S(1)} %get-tuple-element.51), channel_id=1, source_target_pairs={{252,0},{0,4},{4,8},{8,12},{12,16},{16,20},{20,24},{24,28},{28,32}... | collective-permute-start | bytes 98312 | tf_op jit(solution)/shard_map/ppermute | solution.py:26
  338.8 11.2 %collective-permute-start.17 = (f32[64,128]{1,0:T(8,128)S(1)}, f32[64,128]{1,0:T(8,128)S(1)}, u32[]{:S(2)}, u32[]{:S(2)}) collective-permute-start(f32[64,128]{1,0:T(8,128)S(1)} %get-tuple-element.50), channel_id=1, source_target_pairs={{4,0},{8,4},{12,8},{16,12},{20,16},{24,20},{28,24},{32,28},{36,32}... | collective-permute-start | bytes 98312 | tf_op jit(solution)/shard_map/ppermute | solution.py:26
  344.0 7.9 %collective-permute-start.19 = (f32[64,128]{1,0:T(8,128)S(1)}, f32[64,128]{1,0:T(8,128)S(1)}, u32[]{:S(2)}, u32[]{:S(2)}) collective-permute-start(f32[64,128]{1,0:T(8,128)S(1)} %get-tuple-element.48), channel_id=1, source_target_pairs={{8,0},{12,4},{16,8},{20,12},{24,16},{28,20},{32,24},{36,28},{40,32... | collective-permute-start | bytes 98312 | tf_op jit(solution)/shard_map/ppermute | solution.py:26
  366.8 11.4 %collective-permute-start.20 = (f32[64,128]{1,0:T(8,128)S(1)}, f32[64,128]{1,0:T(8,128)S(1)}, u32[]{:S(2)}, u32[]{:S(2)}) collective-permute-start(f32[64,128]{1,0:T(8,128)S(1)} %get-tuple-element.47), channel_id=1, source_target_pairs={{252,0},{0,4},{4,8},{8,12},{12,16},{16,20},{20,24},{24,28},{28,32}... | collective-permute-start | bytes 98312 | tf_op jit(solution)/shard_map/ppermute | solution.py:26
  367.8 10.4 %collective-permute-start.21 = (f32[64,128]{1,0:T(8,128)S(1)}, f32[64,128]{1,0:T(8,128)S(1)}, u32[]{:S(2)}, u32[]{:S(2)}) collective-permute-start(f32[64,128]{1,0:T(8,128)S(1)} %get-tuple-element.46), channel_id=1, source_target_pairs={{4,0},{8,4},{12,8},{16,12},{20,16},{24,20},{28,24},{32,28},{36,32}... | collective-permute-start | bytes 98312 | tf_op jit(solution)/shard_map/ppermute | solution.py:26
  389.0 12.0 %collective-permute-start.24 = (f32[64,128]{1,0:T(8,128)S(1)}, f32[64,128]{1,0:T(8,128)S(1)}, u32[]{:S(2)}, u32[]{:S(2)}) collective-permute-start(f32[64,128]{1,0:T(8,128)S(1)} %get-tuple-element.43), channel_id=1, source_target_pairs={{252,0},{0,4},{4,8},{8,12},{12,16},{16,20},{20,24},{24,28},{28,32}... | collective-permute-start | bytes 98312 | tf_op jit(solution)/shard_map/ppermute | solution.py:26
  390.4 10.7 %collective-permute-start.25 = (f32[64,128]{1,0:T(8,128)S(1)}, f32[64,128]{1,0:T(8,128)S(1)}, u32[]{:S(2)}, u32[]{:S(2)}) collective-permute-start(f32[64,128]{1,0:T(8,128)S(1)} %get-tuple-element.42), channel_id=1, source_target_pairs={{4,0},{8,4},{12,8},{16,12},{20,16},{24,20},{28,24},{32,28},{36,32}... | collective-permute-start | bytes 98312 | tf_op jit(solution)/shard_map/ppermute | solution.py:26
  411.8 173.4 %collective-permute-start.28 = (f32[64,128]{1,0:T(8,128)S(1)}, f32[64,128]{1,0:T(8,128)S(1)}, u32[]{:S(2)}, u32[]{:S(2)}) collective-permute-start(f32[64,128]{1,0:T(8,128)S(1)} %get-tuple-element.39), channel_id=1, source_target_pairs={{252,0},{0,4},{4,8},{8,12},{12,16},{16,20},{20,24},{24,28},{28,32}... | collective-permute-start | bytes 98312 | tf_op jit(solution)/shard_map/ppermute | solution.py:26
  576.6 8.7 %collective-permute-start.29 = (f32[64,128]{1,0:T(8,128)S(1)}, f32[64,128]{1,0:T(8,128)S(1)}, u32[]{:S(2)}, u32[]{:S(2)}) collective-permute-start(f32[64,128]{1,0:T(8,128)S(1)} %get-tuple-element.38), channel_id=1, source_target_pairs={{4,0},{8,4},{12,8},{16,12},{20,16},{24,20},{28,24},{32,28},{36,32}... | collective-permute-start | bytes 98312 | tf_op jit(solution)/shard_map/ppermute | solution.py:26
  (33 other events, 279.6 us)
Sparse Core Ops, SparseCore 0:
  390.5 184.1 all-reduce.1
